TPU v7x, 256 devices: a whole 4x4x8 slice. The times are simulated.
256 devices in a mesh: segment: 8 (over x_lo, y), lat: 16 (over z, x_hi), dp: 2 (over core).
Axes of the slice: x: 4 (x_hi: 2, x_lo: 2; x = x_hi * 2 + x_lo), y: 4, z: 8, core: 2. Of those that a mesh axis runs over, the one named last changes fastest.
Arguments:
- initial: bfloat16 [8, 192, 32, 128], P('dp', None, 'lat'), may hold values from -6 to 6
- kernel: bfloat16 [8, 192, 9, 192], P('segment'), may hold values from -0.078125 to 0.078125
- bias: float32 [8, 192], P('segment'), may hold values from -0.6 to 0.6
- cotangent: bfloat16 [2, 8, 192, 32, 128], P(None, 'dp', None, 'lat'), may hold values from -6 to 6
Outputs:
- section_out: bfloat16 [8, 8, 192, 32, 128], P('segment', 'dp', None, 'lat')
- state_adjoint: float32 [8, 8, 192, 32, 128], P('segment', 'dp', None, 'lat')
- kernel_grad: float32 [8, 192, 9, 192], P('segment')
- bias_grad: float32 [8, 192], P('segment')
All inputs are finite; a program needn't handle non-finite values.
Results may differ from a plain program's by a relative error of at most 0.028.
Values may be sent and summed in bfloat16 or wider, within the bound.
A program may use at most 64 MiB of HBM per device.

v0:
```python
import math
import jax
import jax.numpy as jnp
from jax import lax
from jax.sharding import PartitionSpec as P

STEPS = 2


def passed_along(value, axis, steps):
    count = lax.axis_size(axis)
    pairs = [(source, (source + steps) % count) for source in range(count)]
    return lax.ppermute(value, axis, pairs)


def padded_2(block, sides, width):
    for axis, dim in sides:
        count = lax.axis_size(axis)
        forward = [(i, i + 1) for i in range(count - 1)]
        backward = [(target, source) for source, target in forward]
        low = lax.ppermute(
            lax.slice_in_dim(block, block.shape[dim] - width, None, axis=dim), axis, forward
        )
        high = lax.ppermute(lax.slice_in_dim(block, 0, width, axis=dim), axis, backward)
        block = jnp.concatenate([low, block, high], axis=dim)
    return block


def silu_value(values):
    return values / (1.0 + jnp.exp(-values))


def silu_slope(values):
    sigmoid_v = 1.0 / (1.0 + jnp.exp(-values))
    return sigmoid_v * (1.0 + values * (1.0 - sigmoid_v))


def tap_columns(padded):
    band_rows = padded.shape[1] - 2
    pieces = []
    for row_tap in range(3):
        strip = padded[:, row_tap : row_tap + band_rows, :]
        for col_tap in range(3):
            pieces.append(jnp.roll(strip, 1 - col_tap, axis=2))
    stacked = jnp.stack(pieces, axis=0)
    return stacked.reshape(9 * padded.shape[0], band_rows * padded.shape[2])


def back_columns(padded):
    band_rows = padded.shape[1] - 2
    pieces = []
    for row_tap in range(3):
        strip = padded[:, 2 - row_tap : 2 - row_tap + band_rows, :]
        for col_tap in range(3):
            pieces.append(jnp.roll(strip, col_tap - 1, axis=2))
    stacked = jnp.stack(pieces, axis=0)
    return stacked.reshape(9, padded.shape[0], band_rows * padded.shape[2])


def take_slot(buffer, slot):
    return lax.dynamic_index_in_dim(buffer, slot, 0, keepdims=False)


def put_slot(buffer, slot, value, flag):
    previous = lax.dynamic_index_in_dim(buffer, slot, 0, keepdims=False)
    return lax.dynamic_update_index_in_dim(buffer, jnp.where(flag, value, previous), slot, 0)


def per_device(initial, kernel, bias, cotangent):
    segment_count = lax.axis_size("segment")
    position = lax.axis_index("segment")
    before = jnp.mod(position - 1, segment_count)
    after = jnp.mod(position + 1, segment_count)
    micro = initial.shape[0]
    channels = initial.shape[1]
    band_rows = initial.shape[2]
    longitude = initial.shape[3]
    band_shape = (channels, band_rows, longitude)
    applications = STEPS * segment_count
    flat_kernel = kernel[0].reshape(channels, 9 * channels)
    kernel_taps = kernel[0]
    offsets = bias[0][:, None, None]
    cot_flat = cotangent.reshape((STEPS * micro,) + band_shape)
    tick_count = STEPS * (segment_count + micro - 1)

    def plan(moment, where_at):
        phase_span = segment_count + micro - 1
        rollout_step = jnp.floor_divide(moment, phase_span)
        sample = moment - rollout_step * phase_span - where_at
        applied = rollout_step * segment_count + where_at
        active = (moment >= 0) & (rollout_step < STEPS) & (sample >= 0) & (sample < micro)
        return (jnp.clip(sample, 0, micro - 1), applied, active)

    zero_band = jnp.zeros(band_shape, jnp.bfloat16)
    acts_store = jnp.zeros((STEPS * micro, channels, band_rows + 2, longitude), jnp.bfloat16)

    def forward_tick(moment, carry):
        outgoing, arrived, saved_states, acts_kept, last_outputs = carry
        received = passed_along(outgoing, "segment", 1)
        sent_sample, sent_applied, sent_active = plan(moment - 1, before)
        arrived = put_slot(
            arrived, sent_sample, received, sent_active & (sent_applied < applications - 1)
        )
        sample, applied, active = plan(moment, position)
        current = jnp.where(applied == 0, take_slot(initial, sample), take_slot(arrived, sample))
        activated = silu_value(current.astype(jnp.float32)).astype(jnp.bfloat16)
        padded = padded_2(activated, (("lat", 1),), 1)

        def advance(unused):
            branch = jnp.dot(
                flat_kernel, tap_columns(padded), preferred_element_type=jnp.float32
            ).reshape(band_shape)
            return (current.astype(jnp.float32) + branch + offsets).astype(jnp.bfloat16)

        def holding(unused):
            return current

        produced = lax.cond(active, advance, holding, 0)
        slot = jnp.clip(applied // segment_count, 0, STEPS - 1) * micro + sample
        saved_states = put_slot(saved_states, slot, current, active)
        acts_kept = put_slot(acts_kept, slot, padded, active)
        last_outputs = put_slot(
            last_outputs, sample, produced, active & (applied >= applications - segment_count)
        )
        return (produced, arrived, saved_states, acts_kept, last_outputs)

    forward_start = (
        zero_band,
        jnp.zeros((micro,) + band_shape, jnp.bfloat16),
        jnp.zeros((STEPS * micro,) + band_shape, jnp.bfloat16),
        acts_store,
        jnp.zeros((micro,) + band_shape, jnp.bfloat16),
    )
    unused_out, unused_arrived, saved_states, acts_kept, last_outputs = lax.fori_loop(
        0, tick_count, forward_tick, forward_start
    )

    def backward_tick(turn, carry):
        outgoing, arrived, adjoints, kernel_sum, bias_sum = carry
        received = passed_along(outgoing, "segment", -1)
        sent_sample, sent_applied, sent_active = plan(tick_count - turn, after)
        arrived = put_slot(arrived, sent_sample, received, sent_active & (sent_applied >= 1))
        sample, applied, active = plan(tick_count - 1 - turn, position)
        incoming = jnp.where(
            applied == applications - 1,
            take_slot(cot_flat, (STEPS - 1) * micro + sample),
            take_slot(arrived, sample),
        )
        incoming_padded = padded_2(incoming, (("lat", 1),), 1)
        slot = jnp.clip(applied // segment_count, 0, STEPS - 1) * micro + sample
        current = take_slot(saved_states, slot)
        padded = take_slot(acts_kept, slot)
        step_end = (applied >= segment_count) & (jnp.mod(applied, segment_count) == 0)
        cot_slot = jnp.clip(applied // segment_count - 1, 0, STEPS - 1) * micro + sample

        def retreat(unused):
            gradient_rows = incoming.reshape(channels, band_rows * longitude)
            kernel_term = lax.dot_general(
                gradient_rows,
                tap_columns(padded),
                (((1,), (1,)), ((), ())),
                preferred_element_type=jnp.float32,
            )
            bias_term = jnp.sum(incoming.astype(jnp.float32), axis=(1, 2))
            transposed = lax.dot_general(
                kernel_taps,
                back_columns(incoming_padded),
                (((0, 1), (1, 0)), ((), ())),
                preferred_element_type=jnp.float32,
            ).reshape(band_shape)
            adjoint_here = (
                incoming.astype(jnp.float32) + silu_slope(current.astype(jnp.float32)) * transposed
            )
            adjoint_here = adjoint_here + jnp.where(
                step_end, take_slot(cot_flat, cot_slot).astype(jnp.float32), 0.0
            )
            return (kernel_sum + kernel_term, bias_sum + bias_term, adjoint_here)

        def resting(unused):
            return (kernel_sum, bias_sum, jnp.zeros(band_shape, jnp.float32))

        kernel_sum, bias_sum, adjoint_here = lax.cond(active, retreat, resting, 0)
        adjoints = put_slot(adjoints, sample, adjoint_here, active & (applied < segment_count))
        return (adjoint_here.astype(jnp.bfloat16), arrived, adjoints, kernel_sum, bias_sum)

    backward_start = (
        zero_band,
        jnp.zeros((micro,) + band_shape, jnp.bfloat16),
        jnp.zeros((micro,) + band_shape, jnp.float32),
        jnp.zeros((channels, 9 * channels), jnp.float32),
        jnp.zeros((channels,), jnp.float32),
    )
    unused_grad, unused_inbox, adjoints, kernel_sum, bias_sum = lax.fori_loop(
        0, tick_count, backward_tick, backward_start
    )
    kernel_total, bias_total = (
        lax.psum(kernel_sum.astype(jnp.bfloat16), ("lat", "dp")).astype(jnp.float32),
        lax.psum(bias_sum.astype(jnp.bfloat16), ("lat", "dp")).astype(jnp.float32),
    )
    normalizer = 1.0 / math.sqrt(
        micro * lax.axis_size("dp") * band_rows * lax.axis_size("lat") * longitude
    )
    kernel_grad = (kernel_total * normalizer).reshape(1, channels, 9, channels)
    bias_grad = (bias_total * normalizer)[None]
    return (last_outputs[None], adjoints[None], kernel_grad, bias_grad)


def solution(mesh):
    return jax.shard_map(
        per_device,
        mesh=mesh,
        in_specs=(
            P("dp", None, "lat", None),
            P("segment", None, None, None),
            P("segment", None),
            P(None, "dp", None, "lat", None),
        ),
        out_specs=(
            P("segment", "dp", None, "lat", None),
            P("segment", "dp", None, "lat", None),
            P("segment", None, None, None),
            P("segment", None),
        ),
        check_vma=False,
    )
```

profile of v0, /device:TPU:2, one launch (start us, length us, event | category | flops | bytes accessed | tf_op | source)
XLA Modules:
  0.0 2029.5 jit_solution(11901487231347078123)
XLA Ops:
  13.8 500.7 %while.48 = (s32[]{:T(128)}, bf16[192,2,128]{2,1,0:T(2,128)(2,1)}, bf16[4,192,2,128]{3,1,2,0:T(8,128)(2,1)S(1)}, bf16[8,192,2,128]{3,2,1,0:T(2,128)(2,1)}, bf16[...) while((s32[]{:T(128)}, bf16[192,2,128]{2,1,0:T(2,128)(2,1)}, ...), condition=%wide.region_3.4_spmd, body=%wide.region_0.3_spmd.sunk | while | flops 172425280 | bytes 14624630 | solution.py:134
  95.0 11.4 collective-permute-done
  340.8 15.1 collective-permute-done
  460.2 9.1 collective-permute-start.2
  517.5 1142.3 %while.49 = (s32[]{:T(128)}, bf16[192,2,128]{2,1,0:T(2,128)(2,1)}, bf16[4,192,2,128]{3,2,1,0:T(2,128)(2,1)}, f32[4,192,2,128]{3,2,1,0:T(2,128)}, f32[192,1728]{1...) while((s32[]{:T(128)}, bf16[192,2,128]{2,1,0:T(2,128)(2,1)}, ...), condition=%wide.region_8.9_spmd, body=%wide.region_4.8_spmd.sunk | while | flops 343953472 | bytes 20231204 | solution.py:193
  526.7 8.6 collective-permute-start.5
  573.4 9.4 collective-permute-start.5
  594.2 97.0 %collective-permute-done.3 = bf16[192,2,128]{2,1,0:T(2,128)(2,1)S(1)} collective-permute-done((bf16[192,2,128]{2,1,0:T(2,128)(2,1)}, bf16[192,2,128]{2,1,0:T(2,128)(2,1)S(1)}, u32[]{:S(2)}, u32[]{:S(2)}) %collective-permute-start.3) | collective-permute-done | bytes 98336 | tf_op jit(solution)/shard_map/while/body/eval_jaxpr/ppermute | solution.py:13
  704.0 33.2 %conditional.5 = (f32[192,1728]{1,0:T(8,128)S(1)}, f32[192]{0:T(256)S(1)}, f32[192,2,128]{2,1,0:T(2,128)}, bf16[192,2,128]{2,1,0:T(2,128)(2,1)}) conditional(s32[]{:T(128)} %convert_element_type.170, (f32[192,1728]{1,0:T(8,128)S(1)}, f32[192]{0:T(256)S(1)}) %tuple.180, (s32[]{:T(128)}, s32[]{:T(128)}, pred[]{:T(512)}, pred[]{:T(512)}, ...), branch_computations={%region_5.5_spmd, %region_6.7_spmd.clone} | conditional | flops 343216128 | bytes 17083920 | solution.py:182
  749.2 11.7 collective-permute-start.5
  765.0 33.2 %conditional.5 = (f32[192,1728]{1,0:T(8,128)S(1)}, f32[192]{0:T(256)S(1)}, f32[192,2,128]{2,1,0:T(2,128)}, bf16[192,2,128]{2,1,0:T(2,128)(2,1)}) conditional(s32[]{:T(128)} %convert_element_type.170, (f32[192,1728]{1,0:T(8,128)S(1)}, f32[192]{0:T(256)S(1)}) %tuple.180, (s32[]{:T(128)}, s32[]{:T(128)}, pred[]{:T(512)}, pred[]{:T(512)}, ...), branch_computations={%region_5.5_spmd, %region_6.7_spmd.clone} | conditional | flops 343216128 | bytes 17083920 | solution.py:182
  821.1 33.2 %conditional.5 = (f32[192,1728]{1,0:T(8,128)S(1)}, f32[192]{0:T(256)S(1)}, f32[192,2,128]{2,1,0:T(2,128)}, bf16[192,2,128]{2,1,0:T(2,128)(2,1)}) conditional(s32[]{:T(128)} %convert_element_type.170, (f32[192,1728]{1,0:T(8,128)S(1)}, f32[192]{0:T(256)S(1)}) %tuple.180, (s32[]{:T(128)}, s32[]{:T(128)}, pred[]{:T(512)}, pred[]{:T(512)}, ...), branch_computations={%region_5.5_spmd, %region_6.7_spmd.clone} | conditional | flops 343216128 | bytes 17083920 | solution.py:182
  874.7 33.2 %conditional.5 = (f32[192,1728]{1,0:T(8,128)S(1)}, f32[192]{0:T(256)S(1)}, f32[192,2,128]{2,1,0:T(2,128)}, bf16[192,2,128]{2,1,0:T(2,128)(2,1)}) conditional(s32[]{:T(128)} %convert_element_type.170, (f32[192,1728]{1,0:T(8,128)S(1)}, f32[192]{0:T(256)S(1)}) %tuple.180, (s32[]{:T(128)}, s32[]{:T(128)}, pred[]{:T(512)}, pred[]{:T(512)}, ...), branch_computations={%region_5.5_spmd, %region_6.7_spmd.clone} | conditional | flops 343216128 | bytes 17083920 | solution.py:182
  919.8 8.4 collective-permute-start.5
  934.9 33.9 %collective-permute-start.3 = (bf16[192,2,128]{2,1,0:T(2,128)(2,1)}, bf16[192,2,128]{2,1,0:T(2,128)(2,1)S(1)}, u32[]{:S(2)}, u32[]{:S(2)}) collective-permute-start(bf16[192,2,128]{2,1,0:T(2,128)(2,1)} %get-tuple-element.1480), channel_id=1, source_target_pairs={{0,224},{32,0},{64,32},{96,64},{128,96},{160,128},{192,160},{224,1... | collective-permute-start | bytes 294920 | tf_op jit(solution)/shard_map/while/body/eval_jaxpr/ppermute | solution.py:13
  974.5 9.2 collective-permute-start.5
  1014.9 30.2 %collective-permute-start.3 = (bf16[192,2,128]{2,1,0:T(2,128)(2,1)}, bf16[192,2,128]{2,1,0:T(2,128)(2,1)S(1)}, u32[]{:S(2)}, u32[]{:S(2)}) collective-permute-start(bf16[192,2,128]{2,1,0:T(2,128)(2,1)} %get-tuple-element.1480), channel_id=1, source_target_pairs={{0,224},{32,0},{64,32},{96,64},{128,96},{160,128},{192,160},{224,1... | collective-permute-start | bytes 294920 | tf_op jit(solution)/shard_map/while/body/eval_jaxpr/ppermute | solution.py:13
  1087.3 29.7 %collective-permute-start.3 = (bf16[192,2,128]{2,1,0:T(2,128)(2,1)}, bf16[192,2,128]{2,1,0:T(2,128)(2,1)S(1)}, u32[]{:S(2)}, u32[]{:S(2)}) collective-permute-start(bf16[192,2,128]{2,1,0:T(2,128)(2,1)} %get-tuple-element.1480), channel_id=1, source_target_pairs={{0,224},{32,0},{64,32},{96,64},{128,96},{160,128},{192,160},{224,1... | collective-permute-start | bytes 294920 | tf_op jit(solution)/shard_map/while/body/eval_jaxpr/ppermute | solution.py:13
  1145.6 13.3 collective-permute-start.5
  1164.7 30.2 %collective-permute-start.3 = (bf16[192,2,128]{2,1,0:T(2,128)(2,1)}, bf16[192,2,128]{2,1,0:T(2,128)(2,1)S(1)}, u32[]{:S(2)}, u32[]{:S(2)}) collective-permute-start(bf16[192,2,128]{2,1,0:T(2,128)(2,1)} %get-tuple-element.1480), channel_id=1, source_target_pairs={{0,224},{32,0},{64,32},{96,64},{128,96},{160,128},{192,160},{224,1... | collective-permute-start | bytes 294920 | tf_op jit(solution)/shard_map/while/body/eval_jaxpr/ppermute | solution.py:13
  1195.8 94.5 %collective-permute-done.3 = bf16[192,2,128]{2,1,0:T(2,128)(2,1)S(1)} collective-permute-done((bf16[192,2,128]{2,1,0:T(2,128)(2,1)}, bf16[192,2,128]{2,1,0:T(2,128)(2,1)S(1)}, u32[]{:S(2)}, u32[]{:S(2)}) %collective-permute-start.3) | collective-permute-done | bytes 98336 | tf_op jit(solution)/shard_map/while/body/eval_jaxpr/ppermute | solution.py:13
  1293.6 9.2 collective-permute-start.5
  1305.7 33.2 %conditional.5 = (f32[192,1728]{1,0:T(8,128)S(1)}, f32[192]{0:T(256)S(1)}, f32[192,2,128]{2,1,0:T(2,128)}, bf16[192,2,128]{2,1,0:T(2,128)(2,1)}) conditional(s32[]{:T(128)} %convert_element_type.170, (f32[192,1728]{1,0:T(8,128)S(1)}, f32[192]{0:T(256)S(1)}) %tuple.180, (s32[]{:T(128)}, s32[]{:T(128)}, pred[]{:T(512)}, pred[]{:T(512)}, ...), branch_computations={%region_5.5_spmd, %region_6.7_spmd.clone} | conditional | flops 343216128 | bytes 17083920 | solution.py:182
  1360.4 33.2 %conditional.5 = (f32[192,1728]{1,0:T(8,128)S(1)}, f32[192]{0:T(256)S(1)}, f32[192,2,128]{2,1,0:T(2,128)}, bf16[192,2,128]{2,1,0:T(2,128)(2,1)}) conditional(s32[]{:T(128)} %convert_element_type.170, (f32[192,1728]{1,0:T(8,128)S(1)}, f32[192]{0:T(256)S(1)}) %tuple.180, (s32[]{:T(128)}, s32[]{:T(128)}, pred[]{:T(512)}, pred[]{:T(512)}, ...), branch_computations={%region_5.5_spmd, %region_6.7_spmd.clone} | conditional | flops 343216128 | bytes 17083920 | solution.py:182
  1405.6 9.1 collective-permute-start.5
  1417.6 33.2 %conditional.5 = (f32[192,1728]{1,0:T(8,128)S(1)}, f32[192]{0:T(256)S(1)}, f32[192,2,128]{2,1,0:T(2,128)}, bf16[192,2,128]{2,1,0:T(2,128)(2,1)}) conditional(s32[]{:T(128)} %convert_element_type.170, (f32[192,1728]{1,0:T(8,128)S(1)}, f32[192]{0:T(256)S(1)}) %tuple.180, (s32[]{:T(128)}, s32[]{:T(128)}, pred[]{:T(512)}, pred[]{:T(512)}, ...), branch_computations={%region_5.5_spmd, %region_6.7_spmd.clone} | conditional | flops 343216128 | bytes 17083920 | solution.py:182
  1472.3 33.2 %conditional.5 = (f32[192,1728]{1,0:T(8,128)S(1)}, f32[192]{0:T(256)S(1)}, f32[192,2,128]{2,1,0:T(2,128)}, bf16[192,2,128]{2,1,0:T(2,128)(2,1)}) conditional(s32[]{:T(128)} %convert_element_type.170, (f32[192,1728]{1,0:T(8,128)S(1)}, f32[192]{0:T(256)S(1)}) %tuple.180, (s32[]{:T(128)}, s32[]{:T(128)}, pred[]{:T(512)}, pred[]{:T(512)}, ...), branch_computations={%region_5.5_spmd, %region_6.7_spmd.clone} | conditional | flops 343216128 | bytes 17083920 | solution.py:182
  1515.4 9.7 collective-permute-start.5
  1530.8 37.3 %collective-permute-start.3 = (bf16[192,2,128]{2,1,0:T(2,128)(2,1)}, bf16[192,2,128]{2,1,0:T(2,128)(2,1)S(1)}, u32[]{:S(2)}, u32[]{:S(2)}) collective-permute-start(bf16[192,2,128]{2,1,0:T(2,128)(2,1)} %get-tuple-element.1480), channel_id=1, source_target_pairs={{0,224},{32,0},{64,32},{96,64},{128,96},{160,128},{192,160},{224,1... | collective-permute-start | bytes 294920 | tf_op jit(solution)/shard_map/while/body/eval_jaxpr/ppermute | solution.py:13
  1612.2 29.8 %collective-permute-start.3 = (bf16[192,2,128]{2,1,0:T(2,128)(2,1)}, bf16[192,2,128]{2,1,0:T(2,128)(2,1)S(1)}, u32[]{:S(2)}, u32[]{:S(2)}) collective-permute-start(bf16[192,2,128]{2,1,0:T(2,128)(2,1)} %get-tuple-element.1480), channel_id=1, source_target_pairs={{0,224},{32,0},{64,32},{96,64},{128,96},{160,128},{192,160},{224,1... | collective-permute-start | bytes 294920 | tf_op jit(solution)/shard_map/while/body/eval_jaxpr/ppermute | solution.py:13
  1660.8 94.2 %psum.15 = bf16[192]{0:T(256)(128)(2,1)S(1)} all-reduce(bf16[192]{0:T(256)(128)(2,1)S(1)} %convert_element_type.117), channel_id=1, replica_groups=mesh['segment'=8,'lat'=16,'dp'=2] {'lat','dp'}, use_global_device_ids=true, to_apply=%region_10.11 | all-reduce | flops 192 | bytes 768 | tf_op jit(solution)/shard_map/psum | solution.py:198
  1755.5 261.1 %all-reduce.2.cloned.1.call-done = bf16[192,1728]{1,0:T(8,128)(2,1)} async-done(((bf16[192,1728]{1,0:T(8,128)(2,1)}), bf16[192,1728]{1,0:T(8,128)(2,1)}) %all-reduce.2.cloned.1.call-update) | async-done | bytes 663568 | tf_op jit(solution)/shard_map/psum | solution.py:197
  (1374 shorter events, 1215.2 us)
Async XLA Ops:
  7.2 2009.5 %all-reduce.2.cloned.1.call-start = ((), (), s32[]{:S(2)}) async-start(), calls=%async_computation | async-start | bytes 1376256 | tf_op jit(solution)/shard_map/psum | solution.py:197
  92.5 13.8 collective-permute-start
  338.4 17.6 collective-permute-start
  458.9 11.2 collective-permute-start.1
  460.2 11.2 collective-permute-start.2
  525.4 11.5 collective-permute-start.4
  526.7 12.5 collective-permute-start.5
  572.1 12.3 collective-permute-start.4
  573.4 12.0 collective-permute-start.5
  588.9 102.3 %collective-permute-start.3 = (bf16[192,2,128]{2,1,0:T(2,128)(2,1)}, bf16[192,2,128]{2,1,0:T(2,128)(2,1)S(1)}, u32[]{:S(2)}, u32[]{:S(2)}) collective-permute-start(bf16[192,2,128]{2,1,0:T(2,128)(2,1)} %get-tuple-element.1480), channel_id=1, source_target_pairs={{0,224},{32,0},{64,32},{96,64},{128,96},{160,128},{192,160},{224,1... | collective-permute-start | bytes 294920 | tf_op jit(solution)/shard_map/while/body/eval_jaxpr/ppermute | solution.py:13
  747.9 14.6 collective-permute-start.4
  749.2 15.5 collective-permute-start.5
  918.5 11.4 collective-permute-start.4
  919.8 11.6 collective-permute-start.5
  934.9 36.4 %collective-permute-start.3 = (bf16[192,2,128]{2,1,0:T(2,128)(2,1)}, bf16[192,2,128]{2,1,0:T(2,128)(2,1)S(1)}, u32[]{:S(2)}, u32[]{:S(2)}) collective-permute-start(bf16[192,2,128]{2,1,0:T(2,128)(2,1)} %get-tuple-element.1480), channel_id=1, source_target_pairs={{0,224},{32,0},{64,32},{96,64},{128,96},{160,128},{192,160},{224,1... | collective-permute-start | bytes 294920 | tf_op jit(solution)/shard_map/while/body/eval_jaxpr/ppermute | solution.py:13
  973.2 12.1 collective-permute-start.4
  974.5 11.4 collective-permute-start.5
  1014.9 32.7 %collective-permute-start.3 = (bf16[192,2,128]{2,1,0:T(2,128)(2,1)}, bf16[192,2,128]{2,1,0:T(2,128)(2,1)S(1)}, u32[]{:S(2)}, u32[]{:S(2)}) collective-permute-start(bf16[192,2,128]{2,1,0:T(2,128)(2,1)} %get-tuple-element.1480), channel_id=1, source_target_pairs={{0,224},{32,0},{64,32},{96,64},{128,96},{160,128},{192,160},{224,1... | collective-permute-start | bytes 294920 | tf_op jit(solution)/shard_map/while/body/eval_jaxpr/ppermute | solution.py:13
  1087.3 32.2 %collective-permute-start.3 = (bf16[192,2,128]{2,1,0:T(2,128)(2,1)}, bf16[192,2,128]{2,1,0:T(2,128)(2,1)S(1)}, u32[]{:S(2)}, u32[]{:S(2)}) collective-permute-start(bf16[192,2,128]{2,1,0:T(2,128)(2,1)} %get-tuple-element.1480), channel_id=1, source_target_pairs={{0,224},{32,0},{64,32},{96,64},{128,96},{160,128},{192,160},{224,1... | collective-permute-start | bytes 294920 | tf_op jit(solution)/shard_map/while/body/eval_jaxpr/ppermute | solution.py:13
  1144.3 16.3 collective-permute-start.4
  1145.6 15.5 collective-permute-start.5
  1164.7 125.7 %collective-permute-start.3 = (bf16[192,2,128]{2,1,0:T(2,128)(2,1)}, bf16[192,2,128]{2,1,0:T(2,128)(2,1)S(1)}, u32[]{:S(2)}, u32[]{:S(2)}) collective-permute-start(bf16[192,2,128]{2,1,0:T(2,128)(2,1)} %get-tuple-element.1480), channel_id=1, source_target_pairs={{0,224},{32,0},{64,32},{96,64},{128,96},{160,128},{192,160},{224,1... | collective-permute-start | bytes 294920 | tf_op jit(solution)/shard_map/while/body/eval_jaxpr/ppermute | solution.py:13
  1292.3 12.1 collective-permute-start.4
  1293.6 11.7 collective-permute-start.5
  1404.3 12.0 collective-permute-start.4
  1405.6 11.6 collective-permute-start.5
  1514.1 12.6 collective-permute-start.4
  1515.4 11.8 collective-permute-start.5
  1530.8 39.8 %collective-permute-start.3 = (bf16[192,2,128]{2,1,0:T(2,128)(2,1)}, bf16[192,2,128]{2,1,0:T(2,128)(2,1)S(1)}, u32[]{:S(2)}, u32[]{:S(2)}) collective-permute-start(bf16[192,2,128]{2,1,0:T(2,128)(2,1)} %get-tuple-element.1480), channel_id=1, source_target_pairs={{0,224},{32,0},{64,32},{96,64},{128,96},{160,128},{192,160},{224,1... | collective-permute-start | bytes 294920 | tf_op jit(solution)/shard_map/while/body/eval_jaxpr/ppermute | solution.py:13
  1596.0 11.2 collective-permute-start.4
  1597.3 11.4 collective-permute-start.5
  1612.2 32.3 %collective-permute-start.3 = (bf16[192,2,128]{2,1,0:T(2,128)(2,1)}, bf16[192,2,128]{2,1,0:T(2,128)(2,1)S(1)}, u32[]{:S(2)}, u32[]{:S(2)}) collective-permute-start(bf16[192,2,128]{2,1,0:T(2,128)(2,1)} %get-tuple-element.1480), channel_id=1, source_target_pairs={{0,224},{32,0},{64,32},{96,64},{128,96},{160,128},{192,160},{224,1... | collective-permute-start | bytes 294920 | tf_op jit(solution)/shard_map/while/body/eval_jaxpr/ppermute | solution.py:13
  (127 other events, 1089.9 us)
Sparse Core Ops, SparseCore 0:
  1660.9 355.7 all-reduce.1
where the time goes:
time: 2040 us; the launch traced here: 2030 us
  waiting for transfers between devices  671 us (33%)
  starting transfers between devices  631 us (31%)
  local copies, waits for them, and re-layouts  373 us (18%)
  other arithmetic  222 us (11%)
  blocking collectives  94.2 us (5%)
    ppermute x44, waiting for transfers between devices, passed_along(): return lax.ppermute(value, axis, pairs)  362 us
    ppermute x44, starting transfers between devices, padded_2(): lax.ppermute(lax.slice_in_dim(block, block.shape[dim] - width, None, axis...  334 us
    psum x1, waiting for transfers between devices, per_device(): lax.psum(kernel_sum.astype(jnp.bfloat16), ('lat', 'dp')).astype(jnp.float32)  261 us
    ppermute x44, starting transfers between devices, passed_along(): return lax.ppermute(value, axis, pairs)  240 us
    dynamic_slice x132, local copies, waits for them, and re-layouts, put_slot(): previous = lax.dynamic_index_in_dim(buffer, slot, 0, keepdims=False)  105 us
    psum x1, blocking collectives, per_device(): lax.psum(bias_sum.astype(jnp.bfloat16), ('lat', 'dp')).astype(jnp.float32)  94.2 us
    another operation x80, local copies, waits for them, and re-layouts, back_columns(): stacked = jnp.stack(pieces, axis=0)  68.2 us
    concatenate x48, other arithmetic, back_columns(): pieces.append(jnp.roll(strip, col_tap - 1, axis=2))  63.6 us
  transfers between devices with their start and end apart: 133, of which 89 were waited for; matrix products, arithmetic and copies ran while one was open for 6% of the time, Pallas kernels for 0%

commit v1 on v0

--- a/solution.py
+++ b/solution.py
@@ -5,6 +5,11 @@
 from jax.sharding import PartitionSpec as P
 
 STEPS = 2
+
+
+def by_each_axis(x, axis_one, axis_two):
+    inner = lax.psum(x, axis_one)
+    return lax.psum(inner, axis_two)
 
 
 def passed_along(value, axis, steps):
@@ -194,7 +199,7 @@
         0, tick_count, backward_tick, backward_start
     )
     kernel_total, bias_total = (
-        lax.psum(kernel_sum.astype(jnp.bfloat16), ("lat", "dp")).astype(jnp.float32),
+        by_each_axis(kernel_sum.astype(jnp.bfloat16), "dp", "lat").astype(jnp.float32),
         lax.psum(bias_sum.astype(jnp.bfloat16), ("lat", "dp")).astype(jnp.float32),
     )
     normalizer = 1.0 / math.sqrt(

time: 2040 us -> 1970 us (0.966)
  waiting for transfers between devices: 671 us -> 621 us
  blocking collectives: 94.2 us -> 70.6 us
    psum x1 -> x2, waiting for transfers between devices: 261 us -> 211 us  [the longest x1 119 us: by_each_axis(): inner = lax.psum(x, axis_one)]
    psum x1, blocking collectives: 94.2 us -> 70.6 us  [per_device(): lax.psum(bias_sum.astype(jnp.bfloat16), ('lat', 'dp')).astype(jnp.float32)]
  transfers between devices with their start and end apart: 133 -> 134, of which waited for: 89 -> 90; matrix products, arithmetic and copies ran while one was open for 6% -> 6% of each run, Pallas kernels for 0% -> 0%
where the time goes in v1:
time: 1970 us; the launch traced here: 1950 us
  starting transfers between devices  632 us (32%)
  waiting for transfers between devices  621 us (32%)
  local copies, waits for them, and re-layouts  357 us (18%)
  other arithmetic  236 us (12%)
  blocking collectives  70.6 us (4%)
    ppermute x44, waiting for transfers between devices, passed_along(): return lax.ppermute(value, axis, pairs)  363 us
    ppermute x44, starting transfers between devices, padded_2(): lax.ppermute(lax.slice_in_dim(block, block.shape[dim] - width, None, axis...  335 us
    ppermute x44, starting transfers between devices, passed_along(): return lax.ppermute(value, axis, pairs)  240 us
    psum x1, waiting for transfers between devices, by_each_axis(): inner = lax.psum(x, axis_one)  119 us
    dynamic_slice x132, local copies, waits for them, and re-layouts, put_slot(): previous = lax.dynamic_index_in_dim(buffer, slot, 0, keepdims=False)  104 us
    psum x1, waiting for transfers between devices, by_each_axis(): return lax.psum(inner, axis_two)  92.1 us
    dynamic_update_slice x88, other arithmetic, put_slot(): lax.dynamic_update_index_in_dim(buffer, jnp.where(flag, value, previous),...  75.2 us
    psum x1, blocking collectives, per_device(): lax.psum(bias_sum.astype(jnp.bfloat16), ('lat', 'dp')).astype(jnp.float32)  70.6 us
  transfers between devices with their start and end apart: 134, of which 90 were waited for; matrix products, arithmetic and copies ran while one was open for 6% of the time, Pallas kernels for 0%

profile of v1, /device:TPU:2, one launch (start us, length us, event | category | flops | bytes accessed | tf_op | source)
XLA Modules:
  0.0 1954.8 jit_solution(3103073369984927063)
XLA Ops:
  13.4 499.9 %while.48 = (s32[]{:T(128)}, bf16[192,2,128]{2,1,0:T(2,128)(2,1)}, bf16[4,192,2,128]{3,1,2,0:T(8,128)(2,1)S(1)}, bf16[8,192,2,128]{3,2,1,0:T(2,128)(2,1)}, bf16[...) while((s32[]{:T(128)}, bf16[192,2,128]{2,1,0:T(2,128)(2,1)}, ...), condition=%wide.region_3.4_spmd, body=%wide.region_0.3_spmd.sunk | while | flops 172425280 | bytes 14624630 | solution.py:139
  94.3 11.4 collective-permute-done
  340.3 14.6 collective-permute-done
  459.1 9.1 collective-permute-start.2
  516.3 1142.4 %while.49 = (s32[]{:T(128)}, bf16[192,2,128]{2,1,0:T(2,128)(2,1)}, bf16[4,192,2,128]{3,2,1,0:T(2,128)(2,1)}, f32[4,192,2,128]{3,2,1,0:T(2,128)}, f32[192,1728]{1...) while((s32[]{:T(128)}, bf16[192,2,128]{2,1,0:T(2,128)(2,1)}, ...), condition=%wide.region_8.9_spmd, body=%wide.region_4.8_spmd.sunk | while | flops 343953472 | bytes 20231204 | solution.py:198
  525.5 8.5 collective-permute-start.5
  592.5 97.7 %collective-permute-done.3 = bf16[192,2,128]{2,1,0:T(2,128)(2,1)S(1)} collective-permute-done((bf16[192,2,128]{2,1,0:T(2,128)(2,1)}, bf16[192,2,128]{2,1,0:T(2,128)(2,1)S(1)}, u32[]{:S(2)}, u32[]{:S(2)}) %collective-permute-start.3) | collective-permute-done | bytes 98336 | tf_op jit(solution)/shard_map/while/body/eval_jaxpr/ppermute | solution.py:18
  702.9 33.2 %conditional.5 = (f32[192,1728]{1,0:T(8,128)S(1)}, f32[192]{0:T(256)S(1)}, f32[192,2,128]{2,1,0:T(2,128)}, bf16[192,2,128]{2,1,0:T(2,128)(2,1)}) conditional(s32[]{:T(128)} %convert_element_type.170, (f32[192,1728]{1,0:T(8,128)S(1)}, f32[192]{0:T(256)S(1)}) %tuple.180, (s32[]{:T(128)}, s32[]{:T(128)}, pred[]{:T(512)}, pred[]{:T(512)}, ...), branch_computations={%region_5.5_spmd, %region_6.7_spmd.clone} | conditional | flops 343216128 | bytes 17083920 | solution.py:187
  748.0 11.8 collective-permute-start.5
  763.9 33.2 %conditional.5 = (f32[192,1728]{1,0:T(8,128)S(1)}, f32[192]{0:T(256)S(1)}, f32[192,2,128]{2,1,0:T(2,128)}, bf16[192,2,128]{2,1,0:T(2,128)(2,1)}) conditional(s32[]{:T(128)} %convert_element_type.170, (f32[192,1728]{1,0:T(8,128)S(1)}, f32[192]{0:T(256)S(1)}) %tuple.180, (s32[]{:T(128)}, s32[]{:T(128)}, pred[]{:T(512)}, pred[]{:T(512)}, ...), branch_computations={%region_5.5_spmd, %region_6.7_spmd.clone} | conditional | flops 343216128 | bytes 17083920 | solution.py:187
  820.2 33.2 %conditional.5 = (f32[192,1728]{1,0:T(8,128)S(1)}, f32[192]{0:T(256)S(1)}, f32[192,2,128]{2,1,0:T(2,128)}, bf16[192,2,128]{2,1,0:T(2,128)(2,1)}) conditional(s32[]{:T(128)} %convert_element_type.170, (f32[192,1728]{1,0:T(8,128)S(1)}, f32[192]{0:T(256)S(1)}) %tuple.180, (s32[]{:T(128)}, s32[]{:T(128)}, pred[]{:T(512)}, pred[]{:T(512)}, ...), branch_computations={%region_5.5_spmd, %region_6.7_spmd.clone} | conditional | flops 343216128 | bytes 17083920 | solution.py:187
  873.7 33.2 %conditional.5 = (f32[192,1728]{1,0:T(8,128)S(1)}, f32[192]{0:T(256)S(1)}, f32[192,2,128]{2,1,0:T(2,128)}, bf16[192,2,128]{2,1,0:T(2,128)(2,1)}) conditional(s32[]{:T(128)} %convert_element_type.170, (f32[192,1728]{1,0:T(8,128)S(1)}, f32[192]{0:T(256)S(1)}) %tuple.180, (s32[]{:T(128)}, s32[]{:T(128)}, pred[]{:T(512)}, pred[]{:T(512)}, ...), branch_computations={%region_5.5_spmd, %region_6.7_spmd.clone} | conditional | flops 343216128 | bytes 17083920 | solution.py:187
  918.8 8.4 collective-permute-start.5
  933.9 33.9 %collective-permute-start.3 = (bf16[192,2,128]{2,1,0:T(2,128)(2,1)}, bf16[192,2,128]{2,1,0:T(2,128)(2,1)S(1)}, u32[]{:S(2)}, u32[]{:S(2)}) collective-permute-start(bf16[192,2,128]{2,1,0:T(2,128)(2,1)} %get-tuple-element.1480), channel_id=1, source_target_pairs={{0,224},{32,0},{64,32},{96,64},{128,96},{160,128},{192,160},{224,1... | collective-permute-start | bytes 294920 | tf_op jit(solution)/shard_map/while/body/eval_jaxpr/ppermute | solution.py:18
  973.5 9.2 collective-permute-start.5
  1013.8 30.2 %collective-permute-start.3 = (bf16[192,2,128]{2,1,0:T(2,128)(2,1)}, bf16[192,2,128]{2,1,0:T(2,128)(2,1)S(1)}, u32[]{:S(2)}, u32[]{:S(2)}) collective-permute-start(bf16[192,2,128]{2,1,0:T(2,128)(2,1)} %get-tuple-element.1480), channel_id=1, source_target_pairs={{0,224},{32,0},{64,32},{96,64},{128,96},{160,128},{192,160},{224,1... | collective-permute-start | bytes 294920 | tf_op jit(solution)/shard_map/while/body/eval_jaxpr/ppermute | solution.py:18
  1086.3 29.7 %collective-permute-start.3 = (bf16[192,2,128]{2,1,0:T(2,128)(2,1)}, bf16[192,2,128]{2,1,0:T(2,128)(2,1)S(1)}, u32[]{:S(2)}, u32[]{:S(2)}) collective-permute-start(bf16[192,2,128]{2,1,0:T(2,128)(2,1)} %get-tuple-element.1480), channel_id=1, source_target_pairs={{0,224},{32,0},{64,32},{96,64},{128,96},{160,128},{192,160},{224,1... | collective-permute-start | bytes 294920 | tf_op jit(solution)/shard_map/while/body/eval_jaxpr/ppermute | solution.py:18
  1144.6 13.3 collective-permute-start.5
  1163.6 30.2 %collective-permute-start.3 = (bf16[192,2,128]{2,1,0:T(2,128)(2,1)}, bf16[192,2,128]{2,1,0:T(2,128)(2,1)S(1)}, u32[]{:S(2)}, u32[]{:S(2)}) collective-permute-start(bf16[192,2,128]{2,1,0:T(2,128)(2,1)} %get-tuple-element.1480), channel_id=1, source_target_pairs={{0,224},{32,0},{64,32},{96,64},{128,96},{160,128},{192,160},{224,1... | collective-permute-start | bytes 294920 | tf_op jit(solution)/shard_map/while/body/eval_jaxpr/ppermute | solution.py:18
  1194.7 94.5 %collective-permute-done.3 = bf16[192,2,128]{2,1,0:T(2,128)(2,1)S(1)} collective-permute-done((bf16[192,2,128]{2,1,0:T(2,128)(2,1)}, bf16[192,2,128]{2,1,0:T(2,128)(2,1)S(1)}, u32[]{:S(2)}, u32[]{:S(2)}) %collective-permute-start.3) | collective-permute-done | bytes 98336 | tf_op jit(solution)/shard_map/while/body/eval_jaxpr/ppermute | solution.py:18
  1292.5 9.2 collective-permute-start.5
  1304.5 33.2 %conditional.5 = (f32[192,1728]{1,0:T(8,128)S(1)}, f32[192]{0:T(256)S(1)}, f32[192,2,128]{2,1,0:T(2,128)}, bf16[192,2,128]{2,1,0:T(2,128)(2,1)}) conditional(s32[]{:T(128)} %convert_element_type.170, (f32[192,1728]{1,0:T(8,128)S(1)}, f32[192]{0:T(256)S(1)}) %tuple.180, (s32[]{:T(128)}, s32[]{:T(128)}, pred[]{:T(512)}, pred[]{:T(512)}, ...), branch_computations={%region_5.5_spmd, %region_6.7_spmd.clone} | conditional | flops 343216128 | bytes 17083920 | solution.py:187
  1359.3 33.2 %conditional.5 = (f32[192,1728]{1,0:T(8,128)S(1)}, f32[192]{0:T(256)S(1)}, f32[192,2,128]{2,1,0:T(2,128)}, bf16[192,2,128]{2,1,0:T(2,128)(2,1)}) conditional(s32[]{:T(128)} %convert_element_type.170, (f32[192,1728]{1,0:T(8,128)S(1)}, f32[192]{0:T(256)S(1)}) %tuple.180, (s32[]{:T(128)}, s32[]{:T(128)}, pred[]{:T(512)}, pred[]{:T(512)}, ...), branch_computations={%region_5.5_spmd, %region_6.7_spmd.clone} | conditional | flops 343216128 | bytes 17083920 | solution.py:187
  1404.5 9.1 collective-permute-start.5
  1416.5 33.2 %conditional.5 = (f32[192,1728]{1,0:T(8,128)S(1)}, f32[192]{0:T(256)S(1)}, f32[192,2,128]{2,1,0:T(2,128)}, bf16[192,2,128]{2,1,0:T(2,128)(2,1)}) conditional(s32[]{:T(128)} %convert_element_type.170, (f32[192,1728]{1,0:T(8,128)S(1)}, f32[192]{0:T(256)S(1)}) %tuple.180, (s32[]{:T(128)}, s32[]{:T(128)}, pred[]{:T(512)}, pred[]{:T(512)}, ...), branch_computations={%region_5.5_spmd, %region_6.7_spmd.clone} | conditional | flops 343216128 | bytes 17083920 | solution.py:187
  1471.2 33.2 %conditional.5 = (f32[192,1728]{1,0:T(8,128)S(1)}, f32[192]{0:T(256)S(1)}, f32[192,2,128]{2,1,0:T(2,128)}, bf16[192,2,128]{2,1,0:T(2,128)(2,1)}) conditional(s32[]{:T(128)} %convert_element_type.170, (f32[192,1728]{1,0:T(8,128)S(1)}, f32[192]{0:T(256)S(1)}) %tuple.180, (s32[]{:T(128)}, s32[]{:T(128)}, pred[]{:T(512)}, pred[]{:T(512)}, ...), branch_computations={%region_5.5_spmd, %region_6.7_spmd.clone} | conditional | flops 343216128 | bytes 17083920 | solution.py:187
  1514.3 9.7 collective-permute-start.5
  1529.7 37.3 %collective-permute-start.3 = (bf16[192,2,128]{2,1,0:T(2,128)(2,1)}, bf16[192,2,128]{2,1,0:T(2,128)(2,1)S(1)}, u32[]{:S(2)}, u32[]{:S(2)}) collective-permute-start(bf16[192,2,128]{2,1,0:T(2,128)(2,1)} %get-tuple-element.1480), channel_id=1, source_target_pairs={{0,224},{32,0},{64,32},{96,64},{128,96},{160,128},{192,160},{224,1... | collective-permute-start | bytes 294920 | tf_op jit(solution)/shard_map/while/body/eval_jaxpr/ppermute | solution.py:18
  1611.1 29.8 %collective-permute-start.3 = (bf16[192,2,128]{2,1,0:T(2,128)(2,1)}, bf16[192,2,128]{2,1,0:T(2,128)(2,1)S(1)}, u32[]{:S(2)}, u32[]{:S(2)}) collective-permute-start(bf16[192,2,128]{2,1,0:T(2,128)(2,1)} %get-tuple-element.1480), channel_id=1, source_target_pairs={{0,224},{32,0},{64,32},{96,64},{128,96},{160,128},{192,160},{224,1... | collective-permute-start | bytes 294920 | tf_op jit(solution)/shard_map/while/body/eval_jaxpr/ppermute | solution.py:18
  1659.7 119.0 %all-reduce.3.cloned.1.call-done = bf16[192,1728]{1,0:T(8,128)(2,1)} async-done(((bf16[192,1728]{1,0:T(8,128)(2,1)}), bf16[192,1728]{1,0:T(8,128)(2,1)}) %all-reduce.3.cloned.1.call-update) | async-done | bytes 663568 | tf_op jit(solution)/shard_map/psum | solution.py:11
  1778.7 70.6 %psum.23 = bf16[192]{0:T(256)(128)(2,1)S(1)} all-reduce(bf16[192]{0:T(256)(128)(2,1)S(1)} %convert_element_type.117), channel_id=1, replica_groups=mesh['segment'=8,'lat'=16,'dp'=2] {'lat','dp'}, use_global_device_ids=true, to_apply=%region_11.12 | all-reduce | flops 192 | bytes 768 | tf_op jit(solution)/shard_map/psum | solution.py:203
  1849.9 92.1 %all-reduce.5.cloned.1.call-done = bf16[192,1728]{1,0:T(8,128)(2,1)} async-done(((bf16[192,1728]{1,0:T(8,128)(2,1)}), bf16[192,1728]{1,0:T(8,128)(2,1)}) %all-reduce.5.cloned.1.call-update) | async-done | bytes 663568 | tf_op jit(solution)/shard_map/psum | solution.py:12
  (1377 shorter events, 1223.4 us)
Async XLA Ops:
  7.2 1771.5 %all-reduce.3.cloned.1.call-start = ((), (), s32[]{:S(2)}) async-start(), calls=%async_computation | async-start | bytes 1376256 | tf_op jit(solution)/shard_map/psum | solution.py:11
  91.9 13.8 collective-permute-start
  337.9 17.0 collective-permute-start
  457.8 11.2 collective-permute-start.1
  459.1 11.1 collective-permute-start.2
  524.2 11.5 collective-permute-start.4
  549.2 11.1 collective-permute-start.5
  587.8 102.3 %collective-permute-start.3 = (bf16[192,2,128]{2,1,0:T(2,128)(2,1)}, bf16[192,2,128]{2,1,0:T(2,128)(2,1)S(1)}, u32[]{:S(2)}, u32[]{:S(2)}) collective-permute-start(bf16[192,2,128]{2,1,0:T(2,128)(2,1)} %get-tuple-element.1480), channel_id=1, source_target_pairs={{0,224},{32,0},{64,32},{96,64},{128,96},{160,128},{192,160},{224,1... | collective-permute-start | bytes 294920 | tf_op jit(solution)/shard_map/while/body/eval_jaxpr/ppermute | solution.py:18
  746.7 14.8 collective-permute-start.4
  748.0 15.5 collective-permute-start.5
  808.9 10.9 collective-permute-start.5
  917.5 11.4 collective-permute-start.4
  918.8 11.6 collective-permute-start.5
  933.9 36.4 %collective-permute-start.3 = (bf16[192,2,128]{2,1,0:T(2,128)(2,1)}, bf16[192,2,128]{2,1,0:T(2,128)(2,1)S(1)}, u32[]{:S(2)}, u32[]{:S(2)}) collective-permute-start(bf16[192,2,128]{2,1,0:T(2,128)(2,1)} %get-tuple-element.1480), channel_id=1, source_target_pairs={{0,224},{32,0},{64,32},{96,64},{128,96},{160,128},{192,160},{224,1... | collective-permute-start | bytes 294920 | tf_op jit(solution)/shard_map/while/body/eval_jaxpr/ppermute | solution.py:18
  972.2 12.1 collective-permute-start.4
  973.5 11.4 collective-permute-start.5
  1013.8 32.7 %collective-permute-start.3 = (bf16[192,2,128]{2,1,0:T(2,128)(2,1)}, bf16[192,2,128]{2,1,0:T(2,128)(2,1)S(1)}, u32[]{:S(2)}, u32[]{:S(2)}) collective-permute-start(bf16[192,2,128]{2,1,0:T(2,128)(2,1)} %get-tuple-element.1480), channel_id=1, source_target_pairs={{0,224},{32,0},{64,32},{96,64},{128,96},{160,128},{192,160},{224,1... | collective-permute-start | bytes 294920 | tf_op jit(solution)/shard_map/while/body/eval_jaxpr/ppermute | solution.py:18
  1086.3 32.2 %collective-permute-start.3 = (bf16[192,2,128]{2,1,0:T(2,128)(2,1)}, bf16[192,2,128]{2,1,0:T(2,128)(2,1)S(1)}, u32[]{:S(2)}, u32[]{:S(2)}) collective-permute-start(bf16[192,2,128]{2,1,0:T(2,128)(2,1)} %get-tuple-element.1480), channel_id=1, source_target_pairs={{0,224},{32,0},{64,32},{96,64},{128,96},{160,128},{192,160},{224,1... | collective-permute-start | bytes 294920 | tf_op jit(solution)/shard_map/while/body/eval_jaxpr/ppermute | solution.py:18
  1143.3 16.2 collective-permute-start.4
  1144.6 15.5 collective-permute-start.5
  1163.6 125.7 %collective-permute-start.3 = (bf16[192,2,128]{2,1,0:T(2,128)(2,1)}, bf16[192,2,128]{2,1,0:T(2,128)(2,1)S(1)}, u32[]{:S(2)}, u32[]{:S(2)}) collective-permute-start(bf16[192,2,128]{2,1,0:T(2,128)(2,1)} %get-tuple-element.1480), channel_id=1, source_target_pairs={{0,224},{32,0},{64,32},{96,64},{128,96},{160,128},{192,160},{224,1... | collective-permute-start | bytes 294920 | tf_op jit(solution)/shard_map/while/body/eval_jaxpr/ppermute | solution.py:18
  1291.2 12.1 collective-permute-start.4
  1292.5 11.7 collective-permute-start.5
  1403.2 12.0 collective-permute-start.4
  1404.5 11.6 collective-permute-start.5
  1513.0 12.6 collective-permute-start.4
  1514.3 11.9 collective-permute-start.5
  1529.7 39.8 %collective-permute-start.3 = (bf16[192,2,128]{2,1,0:T(2,128)(2,1)}, bf16[192,2,128]{2,1,0:T(2,128)(2,1)S(1)}, u32[]{:S(2)}, u32[]{:S(2)}) collective-permute-start(bf16[192,2,128]{2,1,0:T(2,128)(2,1)} %get-tuple-element.1480), channel_id=1, source_target_pairs={{0,224},{32,0},{64,32},{96,64},{128,96},{160,128},{192,160},{224,1... | collective-permute-start | bytes 294920 | tf_op jit(solution)/shard_map/while/body/eval_jaxpr/ppermute | solution.py:18
  1594.9 11.2 collective-permute-start.4
  1596.2 11.4 collective-permute-start.5
  1611.1 32.3 %collective-permute-start.3 = (bf16[192,2,128]{2,1,0:T(2,128)(2,1)}, bf16[192,2,128]{2,1,0:T(2,128)(2,1)S(1)}, u32[]{:S(2)}, u32[]{:S(2)}) collective-permute-start(bf16[192,2,128]{2,1,0:T(2,128)(2,1)} %get-tuple-element.1480), channel_id=1, source_target_pairs={{0,224},{32,0},{64,32},{96,64},{128,96},{160,128},{192,160},{224,1... | collective-permute-start | bytes 294920 | tf_op jit(solution)/shard_map/while/body/eval_jaxpr/ppermute | solution.py:18
  1659.7 282.3 %all-reduce.5.cloned.1.call-start = ((), (), s32[]{:S(2)}) async-start(), calls=%async_computation.1 | async-start | bytes 1376256 | tf_op jit(solution)/shard_map/psum | solution.py:12
  (128 other events, 1104.7 us)
Sparse Core Ops, SparseCore 0:
  1659.8 118.8 all-reduce.2
  1781.3 160.6 all-reduce.4
